TPU v7x, 128 devices: a whole 4x4x4 slice. The times are simulated.
128 devices in a mesh: gy: 8 (over x_hi, y), gx: 16 (over z, x_lo, core).
Axes of the slice: x: 4 (x_hi: 2, x_lo: 2; x = x_hi * 2 + x_lo), y: 4, z: 4, core: 2. Of those that a mesh axis runs over, the one named last changes fastest.
Arguments:
- features: bfloat16 [256, 2048, 256], P('gy', 'gx'), may hold values from -8 to 8
- tissue: int32 [16, 128], P('gy', 'gx'), may hold values 0 or 1
- owner_map: int32 [8, 16, 16, 1], P('gy', 'gx'), may hold values from 0 to 15; in each aligned block of 16 rows (0 to 15, 16 to 31, ..., all dimensions but the last counted through in order) at most 2 rows name the same one
- w_conv: bfloat16 [9, 256, 256], replicated, may hold values from -0.125 to 0.125
- w_stride: bfloat16 [4, 256, 256], replicated, may hold values from -0.1875 to 0.1875
- w_query: float32 [256, 256], replicated, may hold values from -0.375 to 0.375
- w_key: float32 [256, 256], replicated, may hold values from -0.375 to 0.375
- w_value: float32 [256, 256], replicated, may hold values from -0.375 to 0.375
- cotangent: float32 [256], replicated, may hold values from -6 to 6
Outputs:
- embedding: float32 [256], replicated
- input_grad: bfloat16 [256, 2048, 256], P('gy', 'gx')
- conv_grad: float32 [9, 256, 256], replicated
Inputs may be any that keep to these rules, and one draw needn't show every extreme that they name: `owner_map`: among the tiles of one device, no owner index is named more than 2 times.
All inputs are finite; a program needn't handle non-finite values. No bound on the sum of `tissue` on one device may be relied on, other than what follows from the above.
Results may differ from a plain program's by a relative error of at most 0.017.
Values may be sent and summed in bfloat16 or wider, within the bound.
A program may use at most 128 MiB of HBM per device.

v0:
```python
from functools import partial
import math
import jax
import jax.numpy as jnp
from jax import lax
from jax.sharding import PartitionSpec as P

HEADS = 4
CAP = 2
attention_bias = -1.0
loss_scale = 512.0


def extended(block, sides, width):
    for axis, dim in sides:
        count = lax.axis_size(axis)
        forward = [(i, i + 1) for i in range(count - 1)]
        backward = [(target, source) for source, target in forward]
        low = lax.ppermute(
            lax.slice_in_dim(block, block.shape[dim] - width, None, axis=dim), axis, forward
        )
        high = lax.ppermute(lax.slice_in_dim(block, 0, width, axis=dim), axis, backward)
        block = jnp.concatenate([low, block, high], axis=dim)
    return block


def forward_taps(padded, weight, pix_rows, pix_cols):
    channels = padded.shape[2]
    running = jnp.zeros((pix_rows * pix_cols, weight.shape[2]), jnp.float32)
    for tap_index in range(9):
        row_off, col_off = (tap_index // 3, tap_index % 3)
        window = padded[row_off : row_off + pix_rows, col_off : col_off + pix_cols].reshape(
            pix_rows * pix_cols, channels
        )
        running = running + jnp.dot(window, weight[tap_index], preferred_element_type=jnp.float32)
    return running.reshape(pix_rows, pix_cols, weight.shape[2])


def backward_taps(padded, weight, pix_rows, pix_cols):
    channels = padded.shape[2]
    running = jnp.zeros((pix_rows * pix_cols, weight.shape[1]), jnp.float32)
    for tap_index in range(9):
        row_off, col_off = (tap_index // 3, tap_index % 3)
        window = padded[
            2 - row_off : 2 - row_off + pix_rows, 2 - col_off : 2 - col_off + pix_cols
        ].reshape(pix_rows * pix_cols, channels)
        running = running + lax.dot_general(
            window, weight[tap_index], (((1,), (1,)), ((), ())), preferred_element_type=jnp.float32
        )
    return running.reshape(pix_rows, pix_cols, weight.shape[1])


def weight_taps(padded, upstream, pix_rows, pix_cols):
    channels = padded.shape[2]
    flat_up = upstream.reshape(pix_rows * pix_cols, upstream.shape[2])
    pieces = []
    for tap_index in range(9):
        row_off, col_off = (tap_index // 3, tap_index % 3)
        window = padded[row_off : row_off + pix_rows, col_off : col_off + pix_cols].reshape(
            pix_rows * pix_cols, channels
        )
        pieces.append(
            lax.dot_general(
                window, flat_up, (((0,), (0,)), ((), ())), preferred_element_type=jnp.float32
            )
        )
    return jnp.stack(pieces)


def strided_forward(field, weight):
    pix_rows, pix_cols, channels = field.shape
    running = jnp.zeros((pix_rows // 2 * (pix_cols // 2), weight.shape[2]), jnp.float32)
    for tap_index in range(4):
        row_off, col_off = (tap_index // 2, tap_index % 2)
        window = field[row_off::2, col_off::2].reshape(-1, channels)
        running = running + jnp.dot(window, weight[tap_index], preferred_element_type=jnp.float32)
    return running.reshape(pix_rows // 2, pix_cols // 2, weight.shape[2])


def strided_backward(upstream, weight):
    half_rows, half_cols, channels = upstream.shape
    flat_up = upstream.reshape(half_rows * half_cols, channels)
    tap_parts = []
    for tap_index in range(4):
        tap_parts.append(
            lax.dot_general(
                flat_up,
                weight[tap_index],
                (((1,), (1,)), ((), ())),
                preferred_element_type=jnp.float32,
            ).reshape(half_rows, half_cols, -1)
        )
    upper_rows = jnp.stack([tap_parts[0], tap_parts[1]], axis=2)
    bottom = jnp.stack([tap_parts[2], tap_parts[3]], axis=2)
    stacked = jnp.stack([upper_rows, bottom], axis=1)
    return stacked.reshape(2 * half_rows, 2 * half_cols, -1)


def rms_normed(tokens_in):
    return tokens_in * lax.rsqrt(jnp.mean(tokens_in * tokens_in, axis=-1, keepdims=True) + 1e-05)


def silu_slope(values):
    gate_sig = jax.nn.sigmoid(values)
    return gate_sig * (1.0 + values * (1.0 - gate_sig))


def attend(
    query_tokens,
    query_flags,
    query_groups,
    key_tokens,
    key_flags,
    key_groups,
    w_query,
    w_key,
    w_value,
    head_count,
):
    highest = lax.Precision.HIGHEST
    query_count = query_tokens.shape[0]
    key_count = key_tokens.shape[0]
    query_rows = jnp.dot(query_tokens, w_query, precision=highest).reshape(
        query_count, head_count, -1
    )
    key_rows = jnp.dot(key_tokens, w_key, precision=highest).reshape(key_count, head_count, -1)
    value_rows = jnp.dot(key_tokens, w_value, precision=highest).reshape(key_count, head_count, -1)
    scores = jnp.einsum("qhd,khd->hqk", query_rows, key_rows, precision=highest) / math.sqrt(
        query_rows.shape[2]
    )
    allowed = (query_groups[:, None] == key_groups[None, :]).astype(jnp.float32) * key_flags[
        None, :
    ]
    weights = jax.nn.sigmoid(scores + attention_bias) * allowed[None]
    mixed_rows = jnp.einsum("hqk,khd->qhd", weights, value_rows, precision=highest).reshape(
        query_count, -1
    )
    return jnp.dot(query_flags, mixed_rows, precision=highest)


def self_attend(tokens_in, tile_flags, tile_groups, w_query, w_key, w_value, head_count):
    return attend(
        tokens_in,
        tile_flags,
        tile_groups,
        tokens_in,
        tile_flags,
        tile_groups,
        w_query,
        w_key,
        w_value,
        head_count,
    )


def per_device(features, tissue, owner_map, w_conv, w_stride, w_query, w_key, w_value, cotangent):
    pix_rows, pix_cols, channels = features.shape
    tile_rows, tile_cols = tissue.shape
    cell_side = pix_rows // (2 * tile_rows)
    gx_count = lax.axis_size("gx")
    tiles_all = tile_rows * tile_cols * lax.axis_size("gy") * gx_count
    norm_scale = 1.0 / math.sqrt(tiles_all)
    seed_grad = cotangent * (loss_scale * norm_scale)
    padded = extended(features, (("gy", 0), ("gx", 1)), 1)
    pre_act = forward_taps(padded, w_conv, pix_rows, pix_cols)
    pixel_mask = jnp.repeat(
        jnp.repeat(tissue.astype(jnp.float32), 2 * cell_side, axis=0), 2 * cell_side, axis=1
    )[:, :, None]
    summed = (features.astype(jnp.float32) + jax.nn.silu(pre_act) * pixel_mask).astype(jnp.bfloat16)
    reduced = strided_forward(summed, w_stride)
    pooled = (
        reduced.reshape(tile_rows, cell_side, tile_cols, cell_side, channels)
        .mean(axis=(1, 3))
        .reshape(-1, channels)
    )
    normed = rms_normed(pooled).astype(jnp.bfloat16)
    tile_flags = tissue.reshape(-1).astype(jnp.float32)
    owners = owner_map.reshape(-1)
    slot_count = gx_count * CAP
    choose = (owners[:, None] == jnp.arange(gx_count, dtype=jnp.int32)[None, :]).astype(jnp.int32)
    earlier = jnp.cumsum(choose, axis=0) - choose
    rank_in = jnp.sum(earlier * choose, axis=1)
    slot_of = owners * CAP + rank_in
    slot_place = (jnp.arange(slot_count, dtype=jnp.int32)[:, None] == slot_of[None, :]).astype(
        jnp.bfloat16
    )
    sent_tokens = (
        jnp.dot(slot_place, normed, preferred_element_type=jnp.float32)
        .astype(jnp.bfloat16)
        .reshape(gx_count, CAP, channels)
    )
    sent_flags = (
        jnp.dot(slot_place, tile_flags.astype(jnp.bfloat16), preferred_element_type=jnp.float32)
        .astype(jnp.bfloat16)
        .reshape(gx_count, CAP)
    )
    got_tokens, got_flags = (
        lax.all_to_all(sent_tokens, "gx", split_axis=0, concat_axis=0, tiled=True),
        lax.all_to_all(sent_flags, "gx", split_axis=0, concat_axis=0, tiled=True),
    )
    group_tokens = got_tokens.reshape(slot_count, channels).astype(jnp.float32)
    group_flags = got_flags.reshape(slot_count).astype(jnp.float32)
    group_ids = jnp.zeros((slot_count,), jnp.int32)
    group_fn = partial(
        self_attend,
        tile_flags=group_flags,
        tile_groups=group_ids,
        w_query=w_query,
        w_key=w_key,
        w_value=w_value,
        head_count=HEADS,
    )
    partial_sum, pull_group = jax.vjp(group_fn, group_tokens)
    slot_grads = pull_group(seed_grad)[0].astype(jnp.bfloat16).reshape(gx_count, CAP, channels)
    returned = lax.all_to_all(slot_grads, "gx", split_axis=0, concat_axis=0, tiled=True)
    token_grad = lax.dot_general(
        slot_place,
        returned.reshape(slot_count, channels),
        (((0,), (0,)), ((), ())),
        preferred_element_type=jnp.float32,
    )
    embedding = lax.psum(partial_sum, ("gy", "gx")) * norm_scale
    pooled_grad = jax.vjp(rms_normed, pooled)[1](token_grad)[0]
    cell_grad = (
        (pooled_grad / (cell_side * cell_side))
        .astype(jnp.bfloat16)
        .reshape(tile_rows, 1, tile_cols, 1, channels)
    )
    cell_grad = jnp.broadcast_to(
        cell_grad, (tile_rows, cell_side, tile_cols, cell_side, channels)
    ).reshape(pix_rows // 2, pix_cols // 2, channels)
    sum_grad = strided_backward(cell_grad, w_stride)
    pre_grad = (sum_grad * pixel_mask * silu_slope(pre_act)).astype(jnp.bfloat16)
    local_grads = weight_taps(padded, pre_grad, pix_rows, pix_cols)
    grad_pad = extended(pre_grad, (("gy", 0), ("gx", 1)), 1)
    input_grad = (sum_grad + backward_taps(grad_pad, w_conv, pix_rows, pix_cols)).astype(
        jnp.bfloat16
    )
    conv_grad = lax.psum(local_grads, ("gy", "gx"))
    conv_grad = conv_grad / loss_scale
    return (embedding, input_grad, conv_grad)


def solution(mesh):
    in_specs = (
        P("gy", "gx", None),
        P("gy", "gx"),
        P("gy", "gx", None, None),
        P(),
        P(),
        P(),
        P(),
        P(),
        P(),
    )
    out_specs = (P(), P("gy", "gx", None), P())
    return jax.shard_map(
        per_device, mesh=mesh, in_specs=in_specs, out_specs=out_specs, check_vma=False
    )
```

profile of v0, /device:TPU:1, one launch (start us, length us, event | category | flops | bytes accessed | tf_op | source)
XLA Modules:
  0.0 436.3 jit_solution(15999486301501065111)
XLA Ops:
  7.2 3.2 copy.54
  10.4 4.0 collective-permute-start
  17.0 7.2 %all-to-all-start = ((bf16[16,1,2]{2,1,0:T(2,128)(2,1)}), bf16[16,1,2]{2,1,0:T(2,128)(2,1)}, u32[]{:S(2)}, u32[]{:S(2)}) async-start(bf16[16,1,2]{2,1,0:T(2,128)(2,1)} %all_to_all.16), calls=%async_computation | async-start | bytes 16384 | tf_op jit(solution)/shard_map/all_to_all | solution.py:199
  25.3 3.0 fusion.131
  32.7 3.5 collective-permute-start.2
  41.0 4.1 copy.69
  45.0 4.1 copy.61
  52.9 7.1 %pad_maximum_fusion = (bf16[34,129,256]{1,2,0:T(8,128)(2,1)S(1)}, bf16[34,129,256]{1,2,0:T(8,128)(2,1)}) fusion(bf16[34,1,256]{1,2,0:T(8,128)(2,1)} %copy.63, bf16[1,128,256]{1,2,0:T(8,128)(2,1)S(1)} %collective-permute-done.1, bf16[32,128,256]{1,2,0:T(8,128)(2,1)S(1)} %copy.54, bf16[1,128,256]{1,2,0:T(8,128)(2,1)S(1)} %collective-permute-done, ...), kind=kLoop, calls=%fused_computation.17 | loop fusion | flops 17965056 | bytes 6754304 | tf_op jit(solution)/shard_map/concatenate | solution.py:23
  60.0 3.6 fusion.127
  63.6 4.1 copy.70
  67.7 4.1 copy.66
  71.8 2.9 copy.64
  74.7 5.8 %fusion.128 = (bf16[32,128,256]{1,2,0:T(8,128)(2,1)}, bf16[32,128,256]{1,2,0:T(8,128)(2,1)S(1)}, bf16[32,128,256]{1,2,0:T(8,128)(2,1)}) fusion(bf16[34,129,256]{1,2,0:T(8,128)(2,1)} %get-tuple-element.20), kind=kLoop, calls=%fused_computation.195 | loop fusion | bytes 12582912 | tf_op jit(solution)/shard_map/slice | solution.py:32
  80.4 4.1 copy.67
  84.5 2.9 copy.65
  87.4 3.4 copy.59
  108.0 5.3 %slice.187 = bf16[16,64,256]{2,1,0:T(8,128)(2,1)} slice(bf16[32,128,256]{2,1,0:T(8,128)(2,1)S(1)} %add_convert_fusion.1), slice={[1:32:2], [1:128:2], [0:256:1]} | slice | bytes 1048576 | tf_op jit(solution)/shard_map/slice | solution.py:75
  113.3 5.3 %slice.185 = bf16[16,64,256]{2,1,0:T(8,128)(2,1)} slice(bf16[32,128,256]{2,1,0:T(8,128)(2,1)S(1)} %add_convert_fusion.1), slice={[1:32:2], [0:128:2], [0:256:1]} | slice | bytes 1048576 | tf_op jit(solution)/shard_map/slice | solution.py:75
  118.5 5.3 %slice.183 = bf16[16,64,256]{2,1,0:T(8,128)(2,1)} slice(bf16[32,128,256]{2,1,0:T(8,128)(2,1)S(1)} %add_convert_fusion.1), slice={[0:32:2], [1:128:2], [0:256:1]} | slice | bytes 1048576 | tf_op jit(solution)/shard_map/slice | solution.py:75
  123.8 5.3 %slice.181 = bf16[16,64,256]{2,1,0:T(8,128)(2,1)} slice(bf16[32,128,256]{2,1,0:T(8,128)(2,1)S(1)} %add_convert_fusion.1), slice={[0:32:2], [0:128:2], [0:256:1]} | slice | bytes 1048576 | tf_op jit(solution)/shard_map/slice | solution.py:75
  134.4 5.8 %all-to-all-start.1 = ((bf16[16,2,256]{2,1,0:T(2,128)(2,1)}), bf16[16,2,256]{2,1,0:T(2,128)(2,1)S(1)}, u32[]{:S(2)}, u32[]{:S(2)}) async-start(bf16[16,2,256]{2,1,0:T(2,128)(2,1)} %reshape.228), calls=%async_computation.1 | async-start | bytes 32768 | tf_op jit(solution)/shard_map/all_to_all | solution.py:198
  149.3 68.0 %psum.14 = f32[256]{0:T(256)S(1)} all-reduce(f32[256]{0:T(256)S(1)} %bitcast.295), channel_id=1, replica_groups=mesh['gy'=8,'gx'=16] {'gy','gx'}, use_global_device_ids=true, to_apply=%region_4.5 | all-reduce | flops 256 | bytes 2048 | tf_op jit(solution)/shard_map/psum | solution.py:222
  218.9 4.0 all-to-all-start.2
  223.5 5.2 %all-to-all-done.2 = bf16[16,2,256]{2,1,0:T(2,128)(2,1)S(1)} async-done(((bf16[16,2,256]{2,1,0:T(2,128)(2,1)}), bf16[16,2,256]{2,1,0:T(2,128)(2,1)S(1)}, u32[]{:S(2)}, u32[]{:S(2)}) %all-to-all-start.2) | async-done | bytes 16416 | tf_op jit(solution)/shard_map/all_to_all | solution.py:215
  231.3 5.2 %copy.82 = f32[16,2,64,2,256]{4,3,2,1,0:T(2,128)} copy(f32[16,2,64,2,256]{4,2,0,3,1:T(8,128)S(1)} %pad_maximum_fusion.1) | data formatting | bytes 8388608 | tf_op jit(solution)/shard_map/stack | solution.py:95
  236.5 6.2 %reshape.236 = f32[32,128,256]{2,1,0:T(8,128)} reshape(f32[16,2,64,2,256]{4,3,2,1,0:T(2,128)} %copy.82) | data formatting | bytes 8388608 | tf_op jit(solution)/shard_map/reshape | solution.py:96
  242.7 4.3 multiply_convert_fusion.1
  247.1 3.2 fusion.29
  266.6 6.1 %reshape.241 = f32[4096,256]{1,0:T(8,128)} reshape(f32[16,2,64,2,256]{4,3,2,1,0:T(2,128)} %copy.82) | data formatting | bytes 8388608 | tf_op jit(solution)/shard_map/reshape | solution.py:96
  275.3 3.0 collective-permute-start.7
  296.7 129.2 %all-reduce.2.cloned.1.call-done = f32[9,256,256]{2,1,0:T(8,128)} async-done(((f32[9,256,256]{2,1,0:T(8,128)}), f32[9,256,256]{2,1,0:T(8,128)}) %all-reduce.2.cloned.1.call-update) | async-done | bytes 2359312 | tf_op jit(solution)/shard_map/psum | solution.py:239
  425.9 3.3 broadcast_multiply_fusion
  (205 shorter events, 89.6 us)
Async XLA Ops:
  7.2 8.6 %copy-start.31 = (s32[2,8]{1,0:T(2,128)S(1)}, s32[2,8]{1,0:T(2,128)}, u32[]{:S(2)}) copy-start(s32[2,8]{1,0:T(2,128)} %param.10) | copy-start | bytes 196
  7.2 8.7 %copy-start.30 = (s32[1,1,16,1]{2,3,1,0:T(1,128)S(1)}, s32[1,1,16,1]{2,3,1,0:T(1,128)}, u32[]{:S(2)}) copy-start(s32[1,1,16,1]{2,3,1,0:T(1,128)} %param.11) | copy-start | bytes 196
  10.4 42.5 %copy-start.3 = (bf16[32,128,256]{1,2,0:T(8,128)(2,1)}, bf16[32,128,256]{1,2,0:T(8,128)(2,1)S(1)}, u32[]{:S(2)}) copy-start(bf16[32,128,256]{1,2,0:T(8,128)(2,1)S(1)} %copy.54) | copy-start | bytes 6291460
  10.4 14.5 %collective-permute-start = (bf16[1,128,256]{1,2,0:T(8,128)(2,1)S(1)}, bf16[1,128,256]{1,2,0:T(8,128)(2,1)S(1)}, u32[]{:S(2)}, u32[]{:S(2)}) collective-permute-start(bf16[1,128,256]{1,2,0:T(8,128)(2,1)S(1)} %get-tuple-element.29), channel_id=1, source_target_pairs={{0,16},{16,32},{32,48},{48,64},{64,80},{80,96},{96,112},{1,17},{17... | collective-permute-start | bytes 196616 | tf_op jit(solution)/shard_map/ppermute | solution.py:19
  14.5 10.5 %collective-permute-start.1 = (bf16[1,128,256]{1,2,0:T(8,128)(2,1)S(1)}, bf16[1,128,256]{1,2,0:T(8,128)(2,1)S(1)}, u32[]{:S(2)}, u32[]{:S(2)}) collective-permute-start(bf16[1,128,256]{1,2,0:T(8,128)(2,1)S(1)} %get-tuple-element.30), channel_id=1, source_target_pairs={{16,0},{32,16},{48,32},{64,48},{80,64},{96,80},{112,96},{17,1},{33... | collective-permute-start | bytes 196616 | tf_op jit(solution)/shard_map/ppermute | solution.py:22
  16.2 8.1 %copy-start.32 = (s32[16]{0:T(128)}, s32[16]{0:T(128)S(1)}, u32[]{:S(2)}) copy-start(s32[16]{0:T(128)S(1)} %multiply_add_fusion.1) | copy-start | bytes 196
  17.0 117.4 %all-to-all-start = ((bf16[16,1,2]{2,1,0:T(2,128)(2,1)}), bf16[16,1,2]{2,1,0:T(2,128)(2,1)}, u32[]{:S(2)}, u32[]{:S(2)}) async-start(bf16[16,1,2]{2,1,0:T(2,128)(2,1)} %all_to_all.16), calls=%async_computation | async-start | bytes 16384 | tf_op jit(solution)/shard_map/all_to_all | solution.py:199
  25.0 27.9 %copy-start.26 = (bf16[1,128,256]{1,2,0:T(8,128)(2,1)}, bf16[1,128,256]{1,2,0:T(8,128)(2,1)S(1)}, u32[]{:S(2)}) copy-start(bf16[1,128,256]{1,2,0:T(8,128)(2,1)S(1)} %collective-permute-done) | copy-start | bytes 196612
  25.0 27.9 %copy-start.24 = (bf16[1,128,256]{1,2,0:T(8,128)(2,1)}, bf16[1,128,256]{1,2,0:T(8,128)(2,1)S(1)}, u32[]{:S(2)}) copy-start(bf16[1,128,256]{1,2,0:T(8,128)(2,1)S(1)} %collective-permute-done.1) | copy-start | bytes 196612
  32.7 18.3 %collective-permute-start.2 = (bf16[34,1,256]{2,0,1:T(8,128)(2,1)S(1)}, bf16[34,1,256]{2,0,1:T(8,128)(2,1)S(1)}, u32[]{:S(2)}, u32[]{:S(2)}) collective-permute-start(bf16[34,1,256]{2,0,1:T(8,128)(2,1)S(1)} %copy.57), channel_id=1, source_target_pairs={{0,1},{1,2},{2,3},{3,4},{4,5},{5,6},{6,7},{7,8},{8,9},{9,10},{10,1... | collective-permute-start | bytes 52232 | tf_op jit(solution)/shard_map/ppermute | solution.py:19
  36.2 12.9 %collective-permute-start.3 = (bf16[34,1,256]{2,0,1:T(8,128)(2,1)S(1)}, bf16[34,1,256]{2,0,1:T(8,128)(2,1)S(1)}, u32[]{:S(2)}, u32[]{:S(2)}) collective-permute-start(bf16[34,1,256]{2,0,1:T(8,128)(2,1)S(1)} %copy.62), channel_id=1, source_target_pairs={{1,0},{2,1},{3,2},{4,3},{5,4},{6,5},{7,6},{8,7},{9,8},{10,9},{11,1... | collective-permute-start | bytes 52232 | tf_op jit(solution)/shard_map/ppermute | solution.py:22
  60.0 3.6 copy-start.5
  132.3 10.2 %copy-start.23 = (f32[256,256]{1,0:T(8,128)S(1)}, f32[256,256]{1,0:T(8,128)}, u32[]{:S(2)}) copy-start(f32[256,256]{1,0:T(8,128)} %param.14) | copy-start | bytes 786436
  132.4 10.3 %copy-start.22 = (f32[256,256]{1,0:T(8,128)S(1)}, f32[256,256]{1,0:T(8,128)}, u32[]{:S(2)}) copy-start(f32[256,256]{1,0:T(8,128)} %param.15) | copy-start | bytes 786436
  132.4 10.4 %copy-start.21 = (f32[256,256]{1,0:T(8,128)S(1)}, f32[256,256]{1,0:T(8,128)}, u32[]{:S(2)}) copy-start(f32[256,256]{1,0:T(8,128)} %param.16) | copy-start | bytes 786436
  134.4 11.6 %all-to-all-start.1 = ((bf16[16,2,256]{2,1,0:T(2,128)(2,1)}), bf16[16,2,256]{2,1,0:T(2,128)(2,1)S(1)}, u32[]{:S(2)}, u32[]{:S(2)}) async-start(bf16[16,2,256]{2,1,0:T(2,128)(2,1)} %reshape.228), calls=%async_computation.1 | async-start | bytes 32768 | tf_op jit(solution)/shard_map/all_to_all | solution.py:198
  142.9 85.8 %copy-start.33 = (s32[16]{0:T(128)S(1)}, s32[16]{0:T(128)}, u32[]{:S(2)}) copy-start(s32[16]{0:T(128)} %copy-done.32) | copy-start | bytes 196
  146.6 82.5 %copy-start.20 = (bf16[4,256,256]{2,1,0:T(8,128)(2,1)S(1)}, bf16[4,256,256]{2,1,0:T(8,128)(2,1)}, u32[]{:S(2)}) copy-start(bf16[4,256,256]{2,1,0:T(8,128)(2,1)} %param.13) | copy-start | bytes 1572868
  218.9 9.8 %all-to-all-start.2 = ((bf16[16,2,256]{2,1,0:T(2,128)(2,1)}), bf16[16,2,256]{2,1,0:T(2,128)(2,1)S(1)}, u32[]{:S(2)}, u32[]{:S(2)}) async-start(bf16[16,2,256]{2,1,0:T(2,128)(2,1)} %reshape.234), calls=%async_computation.2 | async-start | bytes 32768 | tf_op jit(solution)/shard_map/all_to_all | solution.py:215
  222.9 203.1 %all-reduce.2.cloned.1.call-start = ((), (), s32[]{:S(2)}) async-start(), calls=%async_computation.3 | async-start | bytes 4718592 | tf_op jit(solution)/shard_map/psum | solution.py:239
  242.7 11.1 %copy-start.27 = (bf16[1,128,256]{1,2,0:T(8,128)(2,1)S(1)}, bf16[1,128,256]{1,2,0:T(8,128)(2,1)}, u32[]{:S(2)}) copy-start(bf16[1,128,256]{1,2,0:T(8,128)(2,1)} %copy-done.26) | copy-start | bytes 196612
  242.7 12.5 %slice-start = ((s8[4456448]{0:T(1024)(128)(4,1)}), s8[262144]{0:T(1024)(128)(4,1)S(1)}, s32[]{:S(2)}) async-start(s8[4456448]{0:T(1024)(128)(4,1)} %bitcast.258), calls=%async_computation.4 | async-start | bytes 524288
  247.1 6.7 %copy-start.4 = (bf16[32,128,256]{1,2,0:T(8,128)(2,1)S(1)}, bf16[32,128,256]{1,2,0:T(8,128)(2,1)}, u32[]{:S(2)}) copy-start(bf16[32,128,256]{1,2,0:T(8,128)(2,1)} %copy-done.3) | copy-start | bytes 6291460
  247.1 8.2 %slice-start.1 = ((s8[4456448]{0:T(1024)(128)(4,1)}), s8[4194304]{0:T(1024)(128)(4,1)S(1)}, s32[]{:S(2)}) async-start(s8[4456448]{0:T(1024)(128)(4,1)} %bitcast.258), calls=%async_computation.5 | async-start | bytes 8388608
  247.1 9.9 %slice-start.2 = ((s8[4456448]{0:T(1024)(128)(4,1)}), s8[4194304]{0:T(1024)(128)(4,1)S(1)}, s32[]{:S(2)}) async-start(s8[4456448]{0:T(1024)(128)(4,1)} %bitcast.260), calls=%async_computation.6 | async-start | bytes 8388608
  250.3 22.4 %collective-permute-start.4 = (bf16[1,128,256]{2,1,0:T(8,128)(2,1)S(1)}, bf16[1,128,256]{2,1,0:T(8,128)(2,1)S(1)}, u32[]{:S(2)}, u32[]{:S(2)}) collective-permute-start(bf16[1,128,256]{2,1,0:T(8,128)(2,1)S(1)} %get-tuple-element.25), channel_id=1, source_target_pairs={{0,16},{16,32},{32,48},{48,64},{64,80},{80,96},{96,112},{1,17},{17... | collective-permute-start | bytes 196616 | tf_op jit(solution)/shard_map/ppermute | solution.py:19
  252.4 4.6 %slice-start.3 = ((s8[4456448]{0:T(1024)(128)(4,1)}), s8[262144]{0:T(1024)(128)(4,1)S(1)}, s32[]{:S(2)}) async-start(s8[4456448]{0:T(1024)(128)(4,1)} %bitcast.260), calls=%async_computation.7 | async-start | bytes 524288
  252.4 20.3 %collective-permute-start.5 = (bf16[1,128,256]{2,1,0:T(8,128)(2,1)S(1)}, bf16[1,128,256]{2,1,0:T(8,128)(2,1)S(1)}, u32[]{:S(2)}, u32[]{:S(2)}) collective-permute-start(bf16[1,128,256]{2,1,0:T(8,128)(2,1)S(1)} %get-tuple-element.26), channel_id=1, source_target_pairs={{16,0},{32,16},{48,32},{64,48},{80,64},{96,80},{112,96},{17,1},{33... | collective-permute-start | bytes 196616 | tf_op jit(solution)/shard_map/ppermute | solution.py:22
  272.7 6.6 %collective-permute-start.6 = (bf16[34,1,256]{2,1,0:T(2,128)(2,1)S(1)}, bf16[34,1,256]{2,1,0:T(2,128)(2,1)S(1)}, u32[]{:S(2)}, u32[]{:S(2)}) collective-permute-start(bf16[34,1,256]{2,1,0:T(2,128)(2,1)S(1)} %get-tuple-element.17), channel_id=1, source_target_pairs={{1,0},{2,1},{3,2},{4,3},{5,4},{6,5},{7,6},{8,7},{9,8},{10,9},{11,1... | collective-permute-start | bytes 52232 | tf_op jit(solution)/shard_map/ppermute | solution.py:22
  275.3 4.0 collective-permute-start.7
  284.6 3.5 copy-start.16
  284.6 3.5 copy-start.29
  (18 other events, 33.8 us)
Sparse Core Ops, SparseCore 0:
  272.8 153.1 all-reduce.1
where the time goes:
time: 441 us; the launch traced here: 436 us
  waiting for transfers between devices  137 us (31%)
  local copies, waits for them, and re-layouts  113 us (26%)
  blocking collectives  68 us (15%)
  matrix products  39.9 us (9%)
  starting transfers between devices  37.4 us (8%)
  other arithmetic  26.1 us (6%)
  between operations  15.2 us (3%)
    psum x1, waiting for transfers between devices, per_device(): conv_grad = lax.psum(local_grads, ('gy', 'gx'))  129 us
    psum x1, blocking collectives, per_device(): embedding = lax.psum(partial_sum, ('gy', 'gx')) * norm_scale  68 us
    slice x10, local copies, waits for them, and re-layouts, forward_taps(): padded[row_off:row_off + pix_rows, col_off:col_off + pix_cols]  38.9 us
    slice x4, local copies, waits for them, and re-layouts, strided_forward(): window = field[row_off::2, col_off::2].reshape(-1, channels)  21.1 us
    unnamed x81, local copies, waits for them, and re-layouts  17.7 us
    dot_general x9, matrix products, weight_taps(): lax.dot_general(window, flat_up, (((0,), (0,)), ((), ())), preferred_elem...  15.7 us
    ppermute x4, starting transfers between devices, extended(): lax.ppermute(lax.slice_in_dim(block, block.shape[dim] - width, None, axis...  12.6 us
    reshape x2, local copies, waits for them, and re-layouts, strided_backward(): return stacked.reshape(2 * half_rows, 2 * half_cols, -1)  12.3 us
  transfers between devices with their start and end apart: 12, of which 3 were waited for; matrix products, arithmetic and copies ran while one was open for 30% of the time, Pallas kernels for 0%

commit v1 on v0

--- a/solution.py
+++ b/solution.py
@@ -1,3 +1,4 @@
+import functools
 from functools import partial
 import math
 import jax
@@ -9,6 +10,14 @@
 CAP = 2
 attention_bias = -1.0
 loss_scale = 512.0
+
+
+def _register_regions(tile_in, along_axis, axis_name):
+    local_next = lax.psum(lax.psum(tile_in, axis_name=along_axis), axis_name=axis_name)
+    return local_next
+
+
+lift_patches = functools.partial(_register_regions, along_axis="gx", axis_name="gy")
 
 
 def extended(block, sides, width):
@@ -219,7 +228,7 @@
         (((0,), (0,)), ((), ())),
         preferred_element_type=jnp.float32,
     )
-    embedding = lax.psum(partial_sum, ("gy", "gx")) * norm_scale
+    embedding = lift_patches(partial_sum) * norm_scale
     pooled_grad = jax.vjp(rms_normed, pooled)[1](token_grad)[0]
     cell_grad = (
         (pooled_grad / (cell_side * cell_side))

time: 441 us -> 426 us (0.966)
  blocking collectives: 68 us -> 48.3 us
    psum x1 -> x2, blocking collectives: 68 us -> 48.3 us  [the longest x1 26.9 us: _register_regions(): lax.psum(tile_in, axis_name=along_axis)]
    all_to_all x1, starting transfers between devices: 3.96 us -> 9.06 us  [per_device(): lax.all_to_all(slot_grads, 'gx', split_axis=0, concat_axis=0, tiled=True)]
  transfers between devices with their start and end apart: 12 -> 12, of which waited for: 3 -> 3; matrix products, arithmetic and copies ran while one was open for 30% -> 31% of each run, Pallas kernels for 0% -> 0%
where the time goes in v1:
time: 426 us; the launch traced here: 421 us
  waiting for transfers between devices  137 us (32%)
  local copies, waits for them, and re-layouts  113 us (27%)
  blocking collectives  48.3 us (11%)
  starting transfers between devices  41.6 us (10%)
  matrix products  39.9 us (9%)
  other arithmetic  26.5 us (6%)
  between operations  15.1 us (4%)
    psum x1, waiting for transfers between devices, per_device(): conv_grad = lax.psum(local_grads, ('gy', 'gx'))  129 us
    slice x10, local copies, waits for them, and re-layouts, forward_taps(): padded[row_off:row_off + pix_rows, col_off:col_off + pix_cols]  38.9 us
    psum x1, blocking collectives, _register_regions(): lax.psum(tile_in, axis_name=along_axis)  26.9 us
    psum x1, blocking collectives, _register_regions(): lax.psum(lax.psum(tile_in, axis_name=along_axis), axis_name=axis_name)  21.4 us
    slice x4, local copies, waits for them, and re-layouts, strided_forward(): window = field[row_off::2, col_off::2].reshape(-1, channels)  21.3 us
    unnamed x81, local copies, waits for them, and re-layouts  17.7 us
    dot_general x9, matrix products, weight_taps(): lax.dot_general(window, flat_up, (((0,), (0,)), ((), ())), preferred_elem...  15.7 us
    reshape x2, local copies, waits for them, and re-layouts, strided_backward(): return stacked.reshape(2 * half_rows, 2 * half_cols, -1)  12.2 us
  transfers between devices with their start and end apart: 12, of which 3 were waited for; matrix products, arithmetic and copies ran while one was open for 31% of the time, Pallas kernels for 0%

profile of v1, /device:TPU:1, one launch (start us, length us, event | category | flops | bytes accessed | tf_op | source)
XLA Modules:
  0.0 421.4 jit_solution(16157160374194179427)
XLA Ops:
  7.2 3.2 copy.54
  10.4 4.0 collective-permute-start
  17.0 7.2 %all-to-all-start = ((bf16[16,1,2]{2,1,0:T(2,128)(2,1)}), bf16[16,1,2]{2,1,0:T(2,128)(2,1)}, u32[]{:S(2)}, u32[]{:S(2)}) async-start(bf16[16,1,2]{2,1,0:T(2,128)(2,1)} %all_to_all.16), calls=%async_computation | async-start | bytes 16384 | tf_op jit(solution)/shard_map/all_to_all | solution.py:208
  25.3 3.0 fusion.131
  32.7 3.5 collective-permute-start.2
  40.7 4.1 copy.69
  44.8 4.1 copy.61
  52.7 7.2 %pad_maximum_fusion = (bf16[34,129,256]{1,2,0:T(8,128)(2,1)S(1)}, bf16[34,129,256]{1,2,0:T(8,128)(2,1)}) fusion(bf16[34,1,256]{1,2,0:T(8,128)(2,1)} %copy.63, bf16[1,128,256]{1,2,0:T(8,128)(2,1)S(1)} %collective-permute-done.1, bf16[32,128,256]{1,2,0:T(8,128)(2,1)S(1)} %copy.54, bf16[1,128,256]{1,2,0:T(8,128)(2,1)S(1)} %collective-permute-done, ...), kind=kLoop, calls=%fused_computation.17 | loop fusion | flops 17965056 | bytes 6754304 | tf_op jit(solution)/shard_map/concatenate | solution.py:32
  59.9 3.6 fusion.127
  63.5 4.1 copy.70
  67.6 4.1 copy.66
  71.7 2.9 copy.64
  74.6 5.8 %fusion.128 = (bf16[32,128,256]{1,2,0:T(8,128)(2,1)}, bf16[32,128,256]{1,2,0:T(8,128)(2,1)S(1)}, bf16[32,128,256]{1,2,0:T(8,128)(2,1)}) fusion(bf16[34,129,256]{1,2,0:T(8,128)(2,1)} %get-tuple-element.20), kind=kLoop, calls=%fused_computation.195 | loop fusion | bytes 12582912 | tf_op jit(solution)/shard_map/slice | solution.py:41
  80.3 4.1 copy.67
  87.3 3.4 copy.59
  108.3 5.4 %slice.187 = bf16[16,64,256]{2,1,0:T(8,128)(2,1)} slice(bf16[32,128,256]{2,1,0:T(8,128)(2,1)S(1)} %add_convert_fusion.1), slice={[1:32:2], [1:128:2], [0:256:1]} | slice | bytes 1048576 | tf_op jit(solution)/shard_map/slice | solution.py:84
  113.6 5.3 %slice.185 = bf16[16,64,256]{2,1,0:T(8,128)(2,1)} slice(bf16[32,128,256]{2,1,0:T(8,128)(2,1)S(1)} %add_convert_fusion.1), slice={[1:32:2], [0:128:2], [0:256:1]} | slice | bytes 1048576 | tf_op jit(solution)/shard_map/slice | solution.py:84
  118.9 5.3 %slice.183 = bf16[16,64,256]{2,1,0:T(8,128)(2,1)} slice(bf16[32,128,256]{2,1,0:T(8,128)(2,1)S(1)} %add_convert_fusion.1), slice={[0:32:2], [1:128:2], [0:256:1]} | slice | bytes 1048576 | tf_op jit(solution)/shard_map/slice | solution.py:84
  124.2 5.3 %slice.181 = bf16[16,64,256]{2,1,0:T(8,128)(2,1)} slice(bf16[32,128,256]{2,1,0:T(8,128)(2,1)S(1)} %add_convert_fusion.1), slice={[0:32:2], [0:128:2], [0:256:1]} | slice | bytes 1048576 | tf_op jit(solution)/shard_map/slice | solution.py:84
  134.8 5.8 %all-to-all-start.1 = ((bf16[16,2,256]{2,1,0:T(2,128)(2,1)}), bf16[16,2,256]{2,1,0:T(2,128)(2,1)S(1)}, u32[]{:S(2)}, u32[]{:S(2)}) async-start(bf16[16,2,256]{2,1,0:T(2,128)(2,1)} %reshape.228), calls=%async_computation.1 | async-start | bytes 32768 | tf_op jit(solution)/shard_map/all_to_all | solution.py:207
  149.6 26.9 %psum.21 = f32[256]{0:T(256)S(1)} all-reduce(f32[256]{0:T(256)S(1)} %bitcast.295), channel_id=1, replica_groups=mesh['gy'=8,'gx'=16] {'gx'}, use_global_device_ids=true, to_apply=%region_4.5 | all-reduce | flops 256 | bytes 2048 | tf_op jit(solution)/shard_map/psum | solution.py:16
  176.5 21.4 %psum.22 = f32[256]{0:T(256)S(1)} all-reduce(f32[256]{0:T(256)S(1)} %psum.21), channel_id=1, replica_groups=mesh['gy'=8,'gx'=16] {'gy'}, use_global_device_ids=true, to_apply=%region_5.6 | all-reduce | flops 256 | bytes 2048 | tf_op jit(solution)/shard_map/psum | solution.py:16
  199.6 9.1 %all-to-all-start.2 = ((bf16[16,2,256]{2,1,0:T(2,128)(2,1)}), bf16[16,2,256]{2,1,0:T(2,128)(2,1)S(1)}, u32[]{:S(2)}, u32[]{:S(2)}) async-start(bf16[16,2,256]{2,1,0:T(2,128)(2,1)} %reshape.234), calls=%async_computation.2 | async-start | bytes 32768 | tf_op jit(solution)/shard_map/all_to_all | solution.py:224
  209.3 5.2 %all-to-all-done.2 = bf16[16,2,256]{2,1,0:T(2,128)(2,1)S(1)} async-done(((bf16[16,2,256]{2,1,0:T(2,128)(2,1)}), bf16[16,2,256]{2,1,0:T(2,128)(2,1)S(1)}, u32[]{:S(2)}, u32[]{:S(2)}) %all-to-all-start.2) | async-done | bytes 16416 | tf_op jit(solution)/shard_map/all_to_all | solution.py:224
  217.1 5.2 %copy.82 = f32[16,2,64,2,256]{4,3,2,1,0:T(2,128)} copy(f32[16,2,64,2,256]{4,2,0,3,1:T(8,128)S(1)} %pad_maximum_fusion.1) | data formatting | bytes 8388608 | tf_op jit(solution)/shard_map/stack | solution.py:104
  222.4 6.2 %reshape.236 = f32[32,128,256]{2,1,0:T(8,128)} reshape(f32[16,2,64,2,256]{4,3,2,1,0:T(2,128)} %copy.82) | data formatting | bytes 8388608 | tf_op jit(solution)/shard_map/reshape | solution.py:105
  228.6 4.3 %multiply_convert_fusion.1 = bf16[32,128,256]{2,1,0:T(8,128)(2,1)S(1)} fusion(f32[32,128,256]{2,1,0:T(8,128)} %bitcast.257, f32[32,128,256]{2,1,0:T(8,128)} %reshape.236, f32[32,128]{1,0:T(8,128)S(1)} %copy.72), kind=kLoop, calls=%fused_computation.21 | loop fusion | flops 10485760 | bytes 10502144 | tf_op jit(solution)/shard_map/convert_element_type | solution.py:242
  232.9 3.2 fusion.29
  251.7 6.0 %reshape.241 = f32[4096,256]{1,0:T(8,128)} reshape(f32[16,2,64,2,256]{4,3,2,1,0:T(2,128)} %copy.82) | data formatting | bytes 8388608 | tf_op jit(solution)/shard_map/reshape | solution.py:105
  260.2 3.3 collective-permute-start.7
  281.8 129.3 %all-reduce.2.cloned.1.call-done = f32[9,256,256]{2,1,0:T(8,128)} async-done(((f32[9,256,256]{2,1,0:T(8,128)}), f32[9,256,256]{2,1,0:T(8,128)}) %all-reduce.2.cloned.1.call-update) | async-done | bytes 2359312 | tf_op jit(solution)/shard_map/psum | solution.py:248
  411.1 3.3 broadcast_multiply_fusion
  (206 shorter events, 91.6 us)
Async XLA Ops:
  7.2 8.6 %copy-start.31 = (s32[2,8]{1,0:T(2,128)S(1)}, s32[2,8]{1,0:T(2,128)}, u32[]{:S(2)}) copy-start(s32[2,8]{1,0:T(2,128)} %param.10) | copy-start | bytes 196
  7.2 8.7 %copy-start.30 = (s32[1,1,16,1]{2,3,1,0:T(1,128)S(1)}, s32[1,1,16,1]{2,3,1,0:T(1,128)}, u32[]{:S(2)}) copy-start(s32[1,1,16,1]{2,3,1,0:T(1,128)} %param.11) | copy-start | bytes 196
  10.4 42.3 %copy-start.3 = (bf16[32,128,256]{1,2,0:T(8,128)(2,1)}, bf16[32,128,256]{1,2,0:T(8,128)(2,1)S(1)}, u32[]{:S(2)}) copy-start(bf16[32,128,256]{1,2,0:T(8,128)(2,1)S(1)} %copy.54) | copy-start | bytes 6291460
  10.4 14.6 %collective-permute-start = (bf16[1,128,256]{1,2,0:T(8,128)(2,1)S(1)}, bf16[1,128,256]{1,2,0:T(8,128)(2,1)S(1)}, u32[]{:S(2)}, u32[]{:S(2)}) collective-permute-start(bf16[1,128,256]{1,2,0:T(8,128)(2,1)S(1)} %get-tuple-element.29), channel_id=1, source_target_pairs={{0,16},{16,32},{32,48},{48,64},{64,80},{80,96},{96,112},{1,17},{17... | collective-permute-start | bytes 196616 | tf_op jit(solution)/shard_map/ppermute | solution.py:28
  14.5 10.5 %collective-permute-start.1 = (bf16[1,128,256]{1,2,0:T(8,128)(2,1)S(1)}, bf16[1,128,256]{1,2,0:T(8,128)(2,1)S(1)}, u32[]{:S(2)}, u32[]{:S(2)}) collective-permute-start(bf16[1,128,256]{1,2,0:T(8,128)(2,1)S(1)} %get-tuple-element.30), channel_id=1, source_target_pairs={{16,0},{32,16},{48,32},{64,48},{80,64},{96,80},{112,96},{17,1},{33... | collective-permute-start | bytes 196616 | tf_op jit(solution)/shard_map/ppermute | solution.py:31
  16.2 8.1 %copy-start.32 = (s32[16]{0:T(128)}, s32[16]{0:T(128)S(1)}, u32[]{:S(2)}) copy-start(s32[16]{0:T(128)S(1)} %multiply_add_fusion.1) | copy-start | bytes 196
  17.0 117.7 %all-to-all-start = ((bf16[16,1,2]{2,1,0:T(2,128)(2,1)}), bf16[16,1,2]{2,1,0:T(2,128)(2,1)}, u32[]{:S(2)}, u32[]{:S(2)}) async-start(bf16[16,1,2]{2,1,0:T(2,128)(2,1)} %all_to_all.16), calls=%async_computation | async-start | bytes 16384 | tf_op jit(solution)/shard_map/all_to_all | solution.py:208
  25.0 27.7 %copy-start.26 = (bf16[1,128,256]{1,2,0:T(8,128)(2,1)}, bf16[1,128,256]{1,2,0:T(8,128)(2,1)S(1)}, u32[]{:S(2)}) copy-start(bf16[1,128,256]{1,2,0:T(8,128)(2,1)S(1)} %collective-permute-done) | copy-start | bytes 196612
  25.0 27.7 %copy-start.24 = (bf16[1,128,256]{1,2,0:T(8,128)(2,1)}, bf16[1,128,256]{1,2,0:T(8,128)(2,1)S(1)}, u32[]{:S(2)}) copy-start(bf16[1,128,256]{1,2,0:T(8,128)(2,1)S(1)} %collective-permute-done.1) | copy-start | bytes 196612
  32.7 18.1 %collective-permute-start.2 = (bf16[34,1,256]{2,0,1:T(8,128)(2,1)S(1)}, bf16[34,1,256]{2,0,1:T(8,128)(2,1)S(1)}, u32[]{:S(2)}, u32[]{:S(2)}) collective-permute-start(bf16[34,1,256]{2,0,1:T(8,128)(2,1)S(1)} %copy.57), channel_id=1, source_target_pairs={{0,1},{1,2},{2,3},{3,4},{4,5},{5,6},{6,7},{7,8},{8,9},{9,10},{10,1... | collective-permute-start | bytes 52232 | tf_op jit(solution)/shard_map/ppermute | solution.py:28
  36.2 12.6 %collective-permute-start.3 = (bf16[34,1,256]{2,0,1:T(8,128)(2,1)S(1)}, bf16[34,1,256]{2,0,1:T(8,128)(2,1)S(1)}, u32[]{:S(2)}, u32[]{:S(2)}) collective-permute-start(bf16[34,1,256]{2,0,1:T(8,128)(2,1)S(1)} %copy.62), channel_id=1, source_target_pairs={{1,0},{2,1},{3,2},{4,3},{5,4},{6,5},{7,6},{8,7},{9,8},{10,9},{11,1... | collective-permute-start | bytes 52232 | tf_op jit(solution)/shard_map/ppermute | solution.py:31
  59.9 3.6 copy-start.5
  132.7 10.1 %copy-start.23 = (f32[256,256]{1,0:T(8,128)S(1)}, f32[256,256]{1,0:T(8,128)}, u32[]{:S(2)}) copy-start(f32[256,256]{1,0:T(8,128)} %param.14) | copy-start | bytes 786436
  132.8 10.2 %copy-start.22 = (f32[256,256]{1,0:T(8,128)S(1)}, f32[256,256]{1,0:T(8,128)}, u32[]{:S(2)}) copy-start(f32[256,256]{1,0:T(8,128)} %param.15) | copy-start | bytes 786436
  132.8 10.4 %copy-start.21 = (f32[256,256]{1,0:T(8,128)S(1)}, f32[256,256]{1,0:T(8,128)}, u32[]{:S(2)}) copy-start(f32[256,256]{1,0:T(8,128)} %param.16) | copy-start | bytes 786436
  134.8 11.6 %all-to-all-start.1 = ((bf16[16,2,256]{2,1,0:T(2,128)(2,1)}), bf16[16,2,256]{2,1,0:T(2,128)(2,1)S(1)}, u32[]{:S(2)}, u32[]{:S(2)}) async-start(bf16[16,2,256]{2,1,0:T(2,128)(2,1)} %reshape.228), calls=%async_computation.1 | async-start | bytes 32768 | tf_op jit(solution)/shard_map/all_to_all | solution.py:207
  143.3 71.2 %copy-start.33 = (s32[16]{0:T(128)S(1)}, s32[16]{0:T(128)}, u32[]{:S(2)}) copy-start(s32[16]{0:T(128)} %copy-done.32) | copy-start | bytes 196
  147.0 68.0 %copy-start.20 = (bf16[4,256,256]{2,1,0:T(8,128)(2,1)S(1)}, bf16[4,256,256]{2,1,0:T(8,128)(2,1)}, u32[]{:S(2)}) copy-start(bf16[4,256,256]{2,1,0:T(8,128)(2,1)} %param.13) | copy-start | bytes 1572868
  199.6 14.9 %all-to-all-start.2 = ((bf16[16,2,256]{2,1,0:T(2,128)(2,1)}), bf16[16,2,256]{2,1,0:T(2,128)(2,1)S(1)}, u32[]{:S(2)}, u32[]{:S(2)}) async-start(bf16[16,2,256]{2,1,0:T(2,128)(2,1)} %reshape.234), calls=%async_computation.2 | async-start | bytes 32768 | tf_op jit(solution)/shard_map/all_to_all | solution.py:224
  208.7 202.4 %all-reduce.2.cloned.1.call-start = ((), (), s32[]{:S(2)}) async-start(), calls=%async_computation.3 | async-start | bytes 4718592 | tf_op jit(solution)/shard_map/psum | solution.py:248
  228.6 10.4 %copy-start.27 = (bf16[1,128,256]{1,2,0:T(8,128)(2,1)S(1)}, bf16[1,128,256]{1,2,0:T(8,128)(2,1)}, u32[]{:S(2)}) copy-start(bf16[1,128,256]{1,2,0:T(8,128)(2,1)} %copy-done.26) | copy-start | bytes 196612
  228.6 11.8 %slice-start = ((s8[4456448]{0:T(1024)(128)(4,1)}), s8[262144]{0:T(1024)(128)(4,1)S(1)}, s32[]{:S(2)}) async-start(s8[4456448]{0:T(1024)(128)(4,1)} %bitcast.258), calls=%async_computation.4 | async-start | bytes 524288
  232.9 6.1 %copy-start.4 = (bf16[32,128,256]{1,2,0:T(8,128)(2,1)S(1)}, bf16[32,128,256]{1,2,0:T(8,128)(2,1)}, u32[]{:S(2)}) copy-start(bf16[32,128,256]{1,2,0:T(8,128)(2,1)} %copy-done.3) | copy-start | bytes 6291460
  232.9 7.5 %slice-start.1 = ((s8[4456448]{0:T(1024)(128)(4,1)}), s8[4194304]{0:T(1024)(128)(4,1)S(1)}, s32[]{:S(2)}) async-start(s8[4456448]{0:T(1024)(128)(4,1)} %bitcast.258), calls=%async_computation.5 | async-start | bytes 8388608
  232.9 9.2 %slice-start.2 = ((s8[4456448]{0:T(1024)(128)(4,1)}), s8[4194304]{0:T(1024)(128)(4,1)S(1)}, s32[]{:S(2)}) async-start(s8[4456448]{0:T(1024)(128)(4,1)} %bitcast.260), calls=%async_computation.6 | async-start | bytes 8388608
  236.1 21.7 %collective-permute-start.4 = (bf16[1,128,256]{2,1,0:T(8,128)(2,1)S(1)}, bf16[1,128,256]{2,1,0:T(8,128)(2,1)S(1)}, u32[]{:S(2)}, u32[]{:S(2)}) collective-permute-start(bf16[1,128,256]{2,1,0:T(8,128)(2,1)S(1)} %get-tuple-element.25), channel_id=1, source_target_pairs={{0,16},{16,32},{32,48},{48,64},{64,80},{80,96},{96,112},{1,17},{17... | collective-permute-start | bytes 196616 | tf_op jit(solution)/shard_map/ppermute | solution.py:28
  237.5 4.6 %slice-start.3 = ((s8[4456448]{0:T(1024)(128)(4,1)}), s8[262144]{0:T(1024)(128)(4,1)S(1)}, s32[]{:S(2)}) async-start(s8[4456448]{0:T(1024)(128)(4,1)} %bitcast.260), calls=%async_computation.7 | async-start | bytes 524288
  237.5 20.3 %collective-permute-start.5 = (bf16[1,128,256]{2,1,0:T(8,128)(2,1)S(1)}, bf16[1,128,256]{2,1,0:T(8,128)(2,1)S(1)}, u32[]{:S(2)}, u32[]{:S(2)}) collective-permute-start(bf16[1,128,256]{2,1,0:T(8,128)(2,1)S(1)} %get-tuple-element.26), channel_id=1, source_target_pairs={{16,0},{32,16},{48,32},{64,48},{80,64},{96,80},{112,96},{17,1},{33... | collective-permute-start | bytes 196616 | tf_op jit(solution)/shard_map/ppermute | solution.py:31
  257.9 6.6 %collective-permute-start.6 = (bf16[34,1,256]{2,1,0:T(2,128)(2,1)S(1)}, bf16[34,1,256]{2,1,0:T(2,128)(2,1)S(1)}, u32[]{:S(2)}, u32[]{:S(2)}) collective-permute-start(bf16[34,1,256]{2,1,0:T(2,128)(2,1)S(1)} %get-tuple-element.17), channel_id=1, source_target_pairs={{1,0},{2,1},{3,2},{4,3},{5,4},{6,5},{7,6},{8,7},{9,8},{10,9},{11,1... | collective-permute-start | bytes 52232 | tf_op jit(solution)/shard_map/ppermute | solution.py:31
  260.2 4.3 %collective-permute-start.7 = (bf16[34,1,256]{2,1,0:T(2,128)(2,1)S(1)}, bf16[34,1,256]{2,1,0:T(2,128)(2,1)S(1)}, u32[]{:S(2)}, u32[]{:S(2)}) collective-permute-start(bf16[34,1,256]{2,1,0:T(2,128)(2,1)S(1)} %get-tuple-element.18), channel_id=1, source_target_pairs={{0,1},{1,2},{2,3},{3,4},{4,5},{5,6},{6,7},{7,8},{8,9},{9,10},{10,1... | collective-permute-start | bytes 52232 | tf_op jit(solution)/shard_map/ppermute | solution.py:28
  269.7 3.5 copy-start.16
  269.7 3.5 copy-start.29
  (18 other events, 33.8 us)
Sparse Core Ops, SparseCore 0:
  257.9 153.1 all-reduce.1
